TPU v7x, 32 devices: a whole 2x2x4 slice. The times are simulated.
32 devices in a mesh: groups: 2 (over y), seq: 4 (over z), strand: 2 (over core), chan: 2 (over x).
Axes of the slice: x: 2, y: 2, z: 4, core: 2. Of those that a mesh axis runs over, the one named last changes fastest.
Arguments:
- seq_in: bfloat16 [2, 6144, 512], P('strand', ('groups', 'seq', 'chan')), parts along dimension 1, may hold values from -6 to 6
- conv_norm: float32 [2, 512], replicated, may hold values from 0.1 to 1.9
- conv_weight: bfloat16 [2, 3, 512, 512], P(None, None, None, ('seq', 'chan')), may hold values from -0.15625 to 0.15625
- ff_norm: float32 [2, 512], replicated, may hold values from 0.1 to 1.9
- up_weight: bfloat16 [2, 512, 2048], P(None, None, ('seq', 'chan')), may hold values from -0.25 to 0.25
- down_weight: bfloat16 [2, 2048, 512], P(None, ('seq', 'chan')), may hold values from -0.125 to 0.125
- head_norm: float32 [512], replicated, may hold values from 0.1 to 1.9
- value_weight: bfloat16 [512, 512], replicated, may hold values from -0.25 to 0.25
- gate_weight: bfloat16 [512, 512], replicated, may hold values from -0.25 to 0.25
- out_weight: bfloat16 [512, 512], replicated, may hold values from -0.25 to 0.25
Outputs:
- strand_out: bfloat16 [2, 6144, 512], P('strand', ('groups', 'seq', 'chan')), parts along dimension 1
There are 2 independent parts, one for each index of `groups`. A program takes and returns all parts, laid end to end along the dimension named above; an argument that names none is the same for every part. Nothing has to cross between parts.
All inputs are finite; a program needn't handle non-finite values.
Results may differ from a plain program's by a relative error of at most 0.015.
Values may be sent and summed in bfloat16 or wider, within the bound.
No kernel may reach another device: no remote copies, remote signals or barrier semaphores. Data moves between devices by JAX's collectives and lax.ppermute only.
A program may use at most 64 MiB of HBM per device.

v0:
```python
import jax
import jax.numpy as jnp
from jax import lax
from jax.sharding import PartitionSpec as P


def passed_along(value, axis, steps):
    count = lax.axis_size(axis)
    initial, last = (max(0, -steps), min(count, count - steps))
    return lax.ppermute(value, axis, [(source, source + steps) for source in range(initial, last)])


def swapped(x, axis, stride):
    return lax.ppermute(x, axis, [(i, i ^ 1 << stride) for i in range(lax.axis_size(axis))])


def normalize(values, gain):
    return values * lax.rsqrt(jnp.mean(values * values, axis=-1, keepdims=True) + 1e-06) * gain


def matmul(left, right):
    return jnp.dot(left, right, preferred_element_type=jnp.float32)


def local(
    seq_in,
    conv_norm,
    conv_weight,
    ff_norm,
    up_weight,
    down_weight,
    head_norm,
    value_weight,
    gate_weight,
    out_weight,
):
    state = seq_in[0].astype(jnp.float32)
    seq_count = lax.axis_size("seq")
    for block in range(conv_weight.shape[0]):
        reach = min(2**block, seq_count // 2)
        normed = normalize(state, conv_norm[block]).astype(jnp.bfloat16)
        before = passed_along(normed, "seq", reach)
        after = passed_along(normed, "seq", -reach)
        piece = lax.all_gather(conv_weight[block], ("seq", "chan"), axis=2, tiled=True)
        total = matmul(before, piece[0]) + matmul(normed, piece[1]) + matmul(after, piece[2])
        conv = total.astype(jnp.bfloat16)
        state = state + conv.astype(jnp.float32)
        mixed = normalize(state, ff_norm[block]).astype(jnp.bfloat16)
        hidden = jax.nn.gelu(
            matmul(mixed, lax.all_gather(up_weight[block], ("seq", "chan"), axis=1, tiled=True))
        ).astype(jnp.bfloat16)
        state = state + matmul(
            hidden, lax.all_gather(down_weight[block], ("seq", "chan"), axis=0, tiled=True)
        )
    final = normalize(state, head_norm).astype(jnp.bfloat16)
    value = matmul(final, value_weight)
    bit_count = (seq_count * lax.axis_size("chan")).bit_length() - 1
    opposite = swapped(final, "strand", 0)
    for digit in range(bit_count):
        opposite = swapped(opposite, ("seq", "chan"), digit)
    opposite = jnp.flip(opposite, 0)
    mirrored = matmul(opposite, gate_weight).astype(jnp.bfloat16)
    gated = (value * jax.nn.sigmoid(mirrored.astype(jnp.float32))).astype(jnp.bfloat16)
    result = matmul(gated, out_weight)
    return result.astype(jnp.bfloat16)[None]


def solution(mesh):
    in_specs = (
        P("strand", ("groups", "seq", "chan"), None),
        P(),
        P(None, None, None, ("seq", "chan")),
        P(),
        P(None, None, ("seq", "chan")),
        P(None, ("seq", "chan"), None),
        P(),
        P(),
        P(),
        P(),
    )
    out_specs = P("strand", ("groups", "seq", "chan"), None)
    return jax.shard_map(local, mesh=mesh, in_specs=in_specs, out_specs=out_specs, check_vma=False)
```

profile of v0, /device:TPU:0, one launch (start us, length us, event | category | flops | bytes accessed | tf_op | source)
XLA Modules:
  0.0 376.3 jit_solution(10085259237027235437)
XLA Ops:
  6.6 1.9 fusion.86
  8.6 1.9 fusion.84
  14.3 5.6 %collective-permute-start = (bf16[384,512]{1,0:T(8,128)(2,1)S(1)}, bf16[384,512]{1,0:T(8,128)(2,1)S(1)}, u32[]{:S(2)}, u32[]{:S(2)}) collective-permute-start(bf16[384,512]{1,0:T(8,128)(2,1)S(1)} %fusion.57), channel_id=1, source_target_pairs={{0,4},{4,8},{8,12},{1,5},{5,9},{9,13},{2,6},{6,10},{10,14},{3,7},{... | collective-permute-start | bytes 1179656 | tf_op jit(solution)/shard_map/ppermute | solution.py:10
  19.9 10.7 %collective-permute-done.1 = bf16[384,512]{1,0:T(8,128)(2,1)S(1)} collective-permute-done((bf16[384,512]{1,0:T(8,128)(2,1)S(1)}, bf16[384,512]{1,0:T(8,128)(2,1)S(1)}, u32[]{:S(2)}, u32[]{:S(2)}) %collective-permute-start.1) | collective-permute-done | bytes 393248 | tf_op jit(solution)/shard_map/ppermute | solution.py:10
  30.6 28.5 %all-gather.13.cloned.1.call-done = bf16[1,3,512,512]{2,3,1,0:T(8,128)(2,1)} async-done(((bf16[1,3,512,64]{2,3,1,0:T(8,128)(2,1)}), bf16[1,3,512,512]{2,3,1,0:T(8,128)(2,1)}) %all-gather.13.cloned.1.call-update) | async-done | bytes 1572880 | tf_op jit(solution)/shard_map/all_gather | solution.py:44
  59.0 1.4 fusion.62
  60.5 1.5 fusion.63
  62.0 1.6 multiply_reduce_fusion.3
  63.6 47.5 %all-gather.15.cloned.1.call-done = bf16[1,512,2048]{2,1,0:T(8,128)(2,1)} async-done(((bf16[1,512,256]{2,1,0:T(8,128)(2,1)}), bf16[1,512,2048]{2,1,0:T(8,128)(2,1)}) %all-gather.15.cloned.1.call-update) | async-done | bytes 2097168 | tf_op jit(solution)/shard_map/all_gather | solution.py:50
  111.0 49.6 %all-gather.17.cloned.1.call-done = bf16[1,2048,512]{2,1,0:T(8,128)(2,1)} async-done(((bf16[1,256,512]{2,1,0:T(8,128)(2,1)}), bf16[1,2048,512]{2,1,0:T(8,128)(2,1)}) %all-gather.17.cloned.1.call-update) | async-done | bytes 2097168 | tf_op jit(solution)/shard_map/all_gather | solution.py:53
  160.7 4.4 %multiply_reduce_fusion.2 = (f32[384]{0:T(512)S(1)}, f32[384,512]{1,0:T(8,128)S(1)}) fusion(f32[384,512]{1,0:T(8,128)S(1)} %get-tuple-element.16, bf16[1,2048,512]{2,1,0:T(8,128)(2,1)} %all-gather.17.cloned.1.call-done, bf16[1,512,2048]{2,1,0:T(8,128)(2,1)} %all-gather.15.cloned.1.call-done, f32[512]{0:T(512)S(1)} %bitcast.91, f32[384]{0:T(512)S(1)} %add_rsqrt_fusion.3), kind=kOutput, calls=%fused_computation.62 | convolution fusion | flops 1618869888 | bytes 5772288 | tf_op jit(solution)/shard_map/dot_general | solution.py:22
  166.5 5.5 %collective-permute-start.2 = (bf16[384,512]{1,0:T(8,128)(2,1)S(1)}, bf16[384,512]{1,0:T(8,128)(2,1)S(1)}, u32[]{:S(2)}, u32[]{:S(2)}) collective-permute-start(bf16[384,512]{1,0:T(8,128)(2,1)S(1)} %multiply_convert_fusion.4), channel_id=1, source_target_pairs={{0,8},{4,12},{1,9},{5,13},{2,10},{6,14},{3,11},{7,15},{16,24},{20,... | collective-permute-start | bytes 1179656 | tf_op jit(solution)/shard_map/ppermute | solution.py:10
  172.0 46.6 %all-gather.19.cloned.1.call-done = bf16[1,3,512,512]{2,3,1,0:T(8,128)(2,1)} async-done(((bf16[1,3,512,64]{2,3,1,0:T(8,128)(2,1)}), bf16[1,3,512,512]{2,3,1,0:T(8,128)(2,1)}) %all-gather.19.cloned.1.call-update) | async-done | bytes 1572880 | tf_op jit(solution)/shard_map/all_gather | solution.py:44
  218.6 1.4 fusion.61
  221.5 1.6 multiply_reduce_fusion.1
  223.1 47.3 %all-gather.21.cloned.1.call-done = bf16[1,512,2048]{2,1,0:T(8,128)(2,1)} async-done(((bf16[1,512,256]{2,1,0:T(8,128)(2,1)}), bf16[1,512,2048]{2,1,0:T(8,128)(2,1)}) %all-gather.21.cloned.1.call-update) | async-done | bytes 2097168 | tf_op jit(solution)/shard_map/all_gather | solution.py:50
  270.4 49.5 %all-gather.23.cloned.1.call-done = bf16[1,2048,512]{2,1,0:T(8,128)(2,1)} async-done(((bf16[1,256,512]{2,1,0:T(8,128)(2,1)}), bf16[1,2048,512]{2,1,0:T(8,128)(2,1)}) %all-gather.23.cloned.1.call-update) | async-done | bytes 2097168 | tf_op jit(solution)/shard_map/all_gather | solution.py:53
  319.9 4.4 %multiply_reduce_fusion = (f32[384]{0:T(512)S(1)}, f32[384,512]{1,0:T(8,128)S(1)}) fusion(f32[384,512]{1,0:T(8,128)S(1)} %get-tuple-element.20, bf16[1,2048,512]{2,1,0:T(8,128)(2,1)} %all-gather.23.cloned.1.call-done, bf16[1,512,2048]{2,1,0:T(8,128)(2,1)} %all-gather.21.cloned.1.call-done, f32[512]{0:T(512)S(1)} %bitcast.90, f32[384]{0:T(512)S(1)} %add_rsqrt_fusion.1), kind=kOutput, calls=%fused_computation.58 | convolution fusion | flops 1618869888 | bytes 5772288 | tf_op jit(solution)/shard_map/dot_general | solution.py:22
  324.5 1.7 collective-permute-done.4
  326.8 10.6 %collective-permute-done.5 = bf16[384,512]{1,0:T(8,128)(2,1)S(1)} collective-permute-done((bf16[384,512]{1,0:T(8,128)(2,1)S(1)}, bf16[384,512]{1,0:T(8,128)(2,1)S(1)}, u32[]{:S(2)}, u32[]{:S(2)}) %collective-permute-start.5) | collective-permute-done | bytes 393248 | tf_op jit(solution)/shard_map/ppermute | solution.py:14
  337.4 1.5 collective-permute-start.6
  338.8 8.8 %collective-permute-done.6 = bf16[384,512]{1,0:T(8,128)(2,1)S(1)} collective-permute-done((bf16[384,512]{1,0:T(8,128)(2,1)S(1)}, bf16[384,512]{1,0:T(8,128)(2,1)S(1)}, u32[]{:S(2)}, u32[]{:S(2)}) %collective-permute-start.6) | collective-permute-done | bytes 393248 | tf_op jit(solution)/shard_map/ppermute | solution.py:14
  347.7 1.8 collective-permute-start.7
  349.5 16.9 %collective-permute-done.7 = bf16[384,512]{1,0:T(8,128)(2,1)S(1)} collective-permute-done((bf16[384,512]{1,0:T(8,128)(2,1)S(1)}, bf16[384,512]{1,0:T(8,128)(2,1)S(1)}, u32[]{:S(2)}, u32[]{:S(2)}) %collective-permute-start.7) | collective-permute-done | bytes 393248 | tf_op jit(solution)/shard_map/ppermute | solution.py:14
  (51 shorter events, 10.5 us)
Async XLA Ops:
  6.5 360.4 %copy-start = (bf16[512,512]{1,0:T(8,128)(2,1)S(1)}, bf16[512,512]{1,0:T(8,128)(2,1)}, u32[]{:S(2)}) copy-start(bf16[512,512]{1,0:T(8,128)(2,1)} %param.18) | copy-start | bytes 1572868
  6.5 4.0 %copy-start.4 = (bf16[2,256,512]{2,1,0:T(8,128)(2,1)S(1)}, bf16[2,256,512]{2,1,0:T(8,128)(2,1)}, u32[]{:S(2)}) copy-start(bf16[2,256,512]{2,1,0:T(8,128)(2,1)} %param.15) | copy-start | bytes 1572868
  6.5 6.1 %copy-start.1 = (bf16[1,384,512]{2,1,0:T(8,128)(2,1)S(1)}, bf16[1,384,512]{2,1,0:T(8,128)(2,1)}, u32[]{:S(2)}) copy-start(bf16[1,384,512]{2,1,0:T(8,128)(2,1)} %param.10) | copy-start | bytes 1179652
  6.5 6.2 %copy-start.5 = (f32[2,512]{1,0:T(2,128)S(1)}, f32[2,512]{1,0:T(2,128)}, u32[]{:S(2)}) copy-start(f32[2,512]{1,0:T(2,128)} %param.11) | copy-start | bytes 12292
  6.5 52.5 %all-gather.13.cloned.1.call-start = ((), (), s32[]{:S(2)}) async-start(), calls=%async_computation | async-start | bytes 1769472 | tf_op jit(solution)/shard_map/all_gather | solution.py:44
  8.5 11.3 %copy-start.6 = (f32[2,512]{1,0:T(2,128)S(1)}, f32[2,512]{1,0:T(2,128)}, u32[]{:S(2)}) copy-start(f32[2,512]{1,0:T(2,128)} %param.13) | copy-start | bytes 12292
  8.5 102.5 %all-gather.15.cloned.1.call-start = ((), (), s32[]{:S(2)}) async-start(), calls=%async_computation.1 | async-start | bytes 2359296 | tf_op jit(solution)/shard_map/all_gather | solution.py:50
  10.5 150.2 %all-gather.17.cloned.1.call-start = ((), (), s32[]{:S(2)}) async-start(), calls=%async_computation.2 | async-start | bytes 2359296 | tf_op jit(solution)/shard_map/all_gather | solution.py:53
  11.4 207.2 %all-gather.19.cloned.1.call-start = ((), (), s32[]{:S(2)}) async-start(), calls=%async_computation.3 | async-start | bytes 1769472 | tf_op jit(solution)/shard_map/all_gather | solution.py:44
  12.0 258.4 %all-gather.21.cloned.1.call-start = ((), (), s32[]{:S(2)}) async-start(), calls=%async_computation.4 | async-start | bytes 2359296 | tf_op jit(solution)/shard_map/all_gather | solution.py:50
  12.6 307.3 %all-gather.23.cloned.1.call-start = ((), (), s32[]{:S(2)}) async-start(), calls=%async_computation.5 | async-start | bytes 2359296 | tf_op jit(solution)/shard_map/all_gather | solution.py:53
  13.0 17.6 %collective-permute-start.1 = (bf16[384,512]{1,0:T(8,128)(2,1)S(1)}, bf16[384,512]{1,0:T(8,128)(2,1)S(1)}, u32[]{:S(2)}, u32[]{:S(2)}) collective-permute-start(bf16[384,512]{1,0:T(8,128)(2,1)S(1)} %fusion.57), channel_id=1, source_target_pairs={{4,0},{8,4},{12,8},{5,1},{9,5},{13,9},{6,2},{10,6},{14,10},{7,3},{... | collective-permute-start | bytes 1179656 | tf_op jit(solution)/shard_map/ppermute | solution.py:10
  14.3 47.7 %collective-permute-start = (bf16[384,512]{1,0:T(8,128)(2,1)S(1)}, bf16[384,512]{1,0:T(8,128)(2,1)S(1)}, u32[]{:S(2)}, u32[]{:S(2)}) collective-permute-start(bf16[384,512]{1,0:T(8,128)(2,1)S(1)} %fusion.57), channel_id=1, source_target_pairs={{0,4},{4,8},{8,12},{1,5},{5,9},{9,13},{2,6},{6,10},{10,14},{3,7},{... | collective-permute-start | bytes 1179656 | tf_op jit(solution)/shard_map/ppermute | solution.py:10
  165.2 54.9 %collective-permute-start.3 = (bf16[384,512]{1,0:T(8,128)(2,1)S(1)}, bf16[384,512]{1,0:T(8,128)(2,1)S(1)}, u32[]{:S(2)}, u32[]{:S(2)}) collective-permute-start(bf16[384,512]{1,0:T(8,128)(2,1)S(1)} %multiply_convert_fusion.4), channel_id=1, source_target_pairs={{8,0},{12,4},{9,1},{13,5},{10,2},{14,6},{11,3},{15,7},{24,16},{28,... | collective-permute-start | bytes 1179656 | tf_op jit(solution)/shard_map/ppermute | solution.py:10
  166.5 55.0 %collective-permute-start.2 = (bf16[384,512]{1,0:T(8,128)(2,1)S(1)}, bf16[384,512]{1,0:T(8,128)(2,1)S(1)}, u32[]{:S(2)}, u32[]{:S(2)}) collective-permute-start(bf16[384,512]{1,0:T(8,128)(2,1)S(1)} %multiply_convert_fusion.4), channel_id=1, source_target_pairs={{0,8},{4,12},{1,9},{5,13},{2,10},{6,14},{3,11},{7,15},{16,24},{20,... | collective-permute-start | bytes 1179656 | tf_op jit(solution)/shard_map/ppermute | solution.py:10
  319.9 4.4 %copy-start.7 = (f32[512]{0:T(512)S(1)}, f32[512]{0:T(512)}, u32[]{:S(2)}) copy-start(f32[512]{0:T(512)} %param.16) | copy-start | bytes 6148
  324.4 1.8 collective-permute-start.4
  326.2 11.2 %collective-permute-start.5 = (bf16[384,512]{1,0:T(8,128)(2,1)S(1)}, bf16[384,512]{1,0:T(8,128)(2,1)S(1)}, u32[]{:S(2)}, u32[]{:S(2)}) collective-permute-start(bf16[384,512]{1,0:T(8,128)(2,1)S(1)} %collective-permute-done.4), channel_id=1, source_target_pairs={{0,1},{1,0},{4,5},{5,4},{8,9},{9,8},{12,13},{13,12},{2,3},{3,2},{6... | collective-permute-start | bytes 1179656 | tf_op jit(solution)/shard_map/ppermute | solution.py:14
  337.4 10.3 %collective-permute-start.6 = (bf16[384,512]{1,0:T(8,128)(2,1)S(1)}, bf16[384,512]{1,0:T(8,128)(2,1)S(1)}, u32[]{:S(2)}, u32[]{:S(2)}) collective-permute-start(bf16[384,512]{1,0:T(8,128)(2,1)S(1)} %collective-permute-done.5), channel_id=1, source_target_pairs={{0,4},{1,5},{4,0},{5,1},{8,12},{9,13},{12,8},{13,9},{2,6},{3,7},{6... | collective-permute-start | bytes 1179656 | tf_op jit(solution)/shard_map/ppermute | solution.py:14
  347.7 18.7 %collective-permute-start.7 = (bf16[384,512]{1,0:T(8,128)(2,1)S(1)}, bf16[384,512]{1,0:T(8,128)(2,1)S(1)}, u32[]{:S(2)}, u32[]{:S(2)}) collective-permute-start(bf16[384,512]{1,0:T(8,128)(2,1)S(1)} %collective-permute-done.6), channel_id=1, source_target_pairs={{0,8},{1,9},{4,12},{5,13},{8,0},{9,1},{12,4},{13,5},{2,10},{3,11},... | collective-permute-start | bytes 1179656 | tf_op jit(solution)/shard_map/ppermute | solution.py:14
  366.9 1.0 copy-start.2
  366.9 1.2 copy-start.3
Sparse Core Ops, SparseCore 0:
  9.6 49.4 all-gather.12
  61.1 49.8 all-gather.14
  113.1 47.4 all-gather.16
  162.7 55.8 all-gather.18
  220.5 49.8 all-gather.20
  272.4 47.4 all-gather.22
where the time goes:
time: 377 us; the launch traced here: 376 us
  waiting for transfers between devices  319 us (85%)
  matrix products  19.5 us (5%)
  starting transfers between devices  17.8 us (5%)
  between operations  13.7 us (4%)
  local copies, waits for them, and re-layouts  5.8 us (2%)
    all_gather x2, waiting for transfers between devices, local(): lax.all_gather(down_weight[block], ('seq', 'chan'), axis=0, tiled=True)  99.1 us
    all_gather x2, waiting for transfers between devices, local(): lax.all_gather(up_weight[block], ('seq', 'chan'), axis=1, tiled=True)  94.8 us
    all_gather x2, waiting for transfers between devices, local(): lax.all_gather(conv_weight[block], ('seq', 'chan'), axis=2, tiled=True)  75.1 us
    ppermute x4, waiting for transfers between devices, swapped(): lax.ppermute(x, axis, [(i, i ^ 1 << stride) for i in range(lax.axis_size(...  38.1 us
    dot_general x10, matrix products, matmul(): return jnp.dot(left, right, preferred_element_type=jnp.float32)  19.5 us
    ppermute x4, starting transfers between devices, passed_along(): lax.ppermute(value, axis, [(source, source + steps) for source in range(i...  13.7 us
    ppermute x4, waiting for transfers between devices, passed_along(): lax.ppermute(value, axis, [(source, source + steps) for source in range(i...  10.7 us
  transfers between devices with their start and end apart: 14, of which 11 were waited for; matrix products, arithmetic and copies ran while one was open for 4% of the time, Pallas kernels for 0%

commit v1 on v0

--- a/solution.py
+++ b/solution.py
@@ -2,6 +2,40 @@
 import jax.numpy as jnp
 from jax import lax
 from jax.sharding import PartitionSpec as P
+
+
+def update_widths(m, array_axis):
+    m = jnp.moveaxis(m, 0, array_axis)
+    plain = m.shape
+    a_now = m.reshape(
+        *plain[:array_axis], plain[array_axis] * plain[array_axis + 1], *plain[array_axis + 2 :]
+    )
+    return a_now
+
+
+def recover_lines(in_array, chip_axis, where_dim):
+    workers = jax.lax.axis_size(chip_axis)
+    parts_seen = [(j0, (j0 + 1) % workers) for j0 in range(workers)]
+    all_rows = [(pp, c) for c, pp in parts_seen]
+    lower, block_last = ([], [])
+    for s in range(workers - 1):
+        if s % 2 == 0:
+            step_out = jax.lax.ppermute(
+                lower[-1] if lower else in_array, chip_axis, perm=parts_seen
+            )
+            lower.append(step_out)
+        else:
+            current_block = jax.lax.ppermute(
+                block_last[-1] if block_last else in_array, chip_axis, all_rows
+            )
+            block_last.append(current_block)
+    placed = jnp.stack([*lower[::-1], in_array, *block_last])
+    small = jax.lax.axis_index(chip_axis)
+    item_now = len(lower)
+    f_next = small - item_now
+    placed = placed[(jnp.arange(workers) - f_next) % workers]
+    reached = update_widths(placed, where_dim)
+    return reached
 
 
 def passed_along(value, axis, steps):
@@ -41,7 +75,7 @@
         normed = normalize(state, conv_norm[block]).astype(jnp.bfloat16)
         before = passed_along(normed, "seq", reach)
         after = passed_along(normed, "seq", -reach)
-        piece = lax.all_gather(conv_weight[block], ("seq", "chan"), axis=2, tiled=True)
+        piece = recover_lines(conv_weight[block], ("seq", "chan"), 2)
         total = matmul(before, piece[0]) + matmul(normed, piece[1]) + matmul(after, piece[2])
         conv = total.astype(jnp.bfloat16)
         state = state + conv.astype(jnp.float32)

time: 377 us -> 314 us (0.83)
  waiting for transfers between devices: 319 us -> 220 us
  starting transfers between devices: 17.8 us -> 40.2 us
  local copies, waits for them, and re-layouts: 5.8 us -> 20.9 us
    all_gather x2 -> x0, waiting for transfers between devices: 75.1 us -> none  [local(): lax.all_gather(conv_weight[block], ('seq', 'chan'), axis=2, tiled=True)]
    all_gather x2, waiting for transfers between devices: 99.1 us -> 49.5 us  [local(): lax.all_gather(down_weight[block], ('seq', 'chan'), axis=0, tiled=True)]
    ppermute x0 -> x14, waiting for transfers between devices: none -> 46.2 us  [the longest x8 46.1 us: recover_lines(): jax.lax.ppermute(lower[-1] if lower else in_array, chip_axis, perm=parts_...]
    all_gather x2, waiting for transfers between devices: 94.8 us -> 64.4 us  [local(): lax.all_gather(up_weight[block], ('seq', 'chan'), axis=1, tiled=True)]
    ppermute x0 -> x14, starting transfers between devices: none -> 26 us  [the longest x6 18.5 us: recover_lines(): jax.lax.ppermute(block_last[-1] if block_last else in_array, chip_axis, a...]
    ppermute x4, waiting for transfers between devices: 10.7 us -> 21.6 us  [passed_along(): lax.ppermute(value, axis, [(source, source + steps) for source in range(i...]
    unnamed x16 -> x33, local copies, waits for them, and re-layouts: 0.73 us -> 9.85 us
    gather x0 -> x2, local copies, waits for them, and re-layouts: none -> 4.17 us  [recover_lines(): placed = placed[(jnp.arange(workers) - f_next) % workers]]
  transfers between devices with their start and end apart: 14 -> 26, of which waited for: 11 -> 14; matrix products, arithmetic and copies ran while one was open for 4% -> 10% of each run, Pallas kernels for 0% -> 0%
where the time goes in v1:
time: 314 us
  waiting for transfers between devices  220 us (70%)
  starting transfers between devices  40.2 us (13%)
  local copies, waits for them, and re-layouts  20.9 us (7%)
  matrix products  17.6 us (6%)
  between operations  13.4 us (4%)
    all_gather x2, waiting for transfers between devices, local(): lax.all_gather(up_weight[block], ('seq', 'chan'), axis=1, tiled=True)  64.4 us
    all_gather x2, waiting for transfers between devices, local(): lax.all_gather(down_weight[block], ('seq', 'chan'), axis=0, tiled=True)  49.5 us
    ppermute x8, waiting for transfers between devices, recover_lines(): jax.lax.ppermute(lower[-1] if lower else in_array, chip_axis, perm=parts_...  46.1 us
    ppermute x4, waiting for transfers between devices, swapped(): lax.ppermute(x, axis, [(i, i ^ 1 << stride) for i in range(lax.axis_size(...  38.1 us
    ppermute x4, waiting for transfers between devices, passed_along(): lax.ppermute(value, axis, [(source, source + steps) for source in range(i...  21.6 us
    ppermute x6, starting transfers between devices, recover_lines(): jax.lax.ppermute(block_last[-1] if block_last else in_array, chip_axis, a...  18.5 us
    dot_general x10, matrix products, matmul(): return jnp.dot(left, right, preferred_element_type=jnp.float32)  17.6 us
    ppermute x4, starting transfers between devices, passed_along(): lax.ppermute(value, axis, [(source, source + steps) for source in range(i...  10.1 us
  transfers between devices with their start and end apart: 26, of which 14 were waited for; matrix products, arithmetic and copies ran while one was open for 10% of the time, Pallas kernels for 0%

profile of v1, /device:TPU:0, one launch (start us, length us, event | category | flops | bytes accessed | tf_op | source)
XLA Modules:
  0.0 313.9 jit_solution(6227814277452824533)
XLA Ops:
  10.3 3.0 collective-permute-start.1
  13.3 3.1 collective-permute-start.5
  16.4 4.7 %collective-permute-start.14 = (bf16[3,512,64]{1,2,0:T(8,128)(2,1)S(1)}, bf16[3,512,64]{1,2,0:T(8,128)(2,1)S(1)}, u32[]{:S(2)}, u32[]{:S(2)}) collective-permute-start(bf16[3,512,64]{1,2,0:T(8,128)(2,1)S(1)} %get-tuple-element.17), channel_id=1, source_target_pairs={{1,0},{4,1},{5,4},{8,5},{9,8},{12,9},{13,12},{0,13},{3,2},{6,3},{7... | collective-permute-start | bytes 589832 | tf_op jit(solution)/shard_map/ppermute | solution.py:28
  21.3 8.5 %collective-permute-done.1 = bf16[3,512,64]{1,2,0:T(8,128)(2,1)S(1)} collective-permute-done((bf16[3,512,64]{1,2,0:T(8,128)(2,1)S(1)}, bf16[3,512,64]{1,2,0:T(8,128)(2,1)S(1)}, u32[]{:S(2)}, u32[]{:S(2)}) %collective-permute-start.1) | collective-permute-done | bytes 196640 | tf_op jit(solution)/shard_map/ppermute | solution.py:23
  29.9 2.5 collective-permute-start.2
  36.6 7.8 %collective-permute-done.2 = bf16[3,512,64]{1,2,0:T(8,128)(2,1)S(1)} collective-permute-done((bf16[3,512,64]{1,2,0:T(8,128)(2,1)S(1)}, bf16[3,512,64]{1,2,0:T(8,128)(2,1)S(1)}, u32[]{:S(2)}, u32[]{:S(2)}) %collective-permute-start.2) | collective-permute-done | bytes 196640 | tf_op jit(solution)/shard_map/ppermute | solution.py:23
  44.4 4.8 %collective-permute-start.6 = (bf16[3,512,64]{1,2,0:T(8,128)(2,1)S(1)}, bf16[3,512,64]{1,2,0:T(8,128)(2,1)S(1)}, u32[]{:S(2)}, u32[]{:S(2)}) collective-permute-start(bf16[3,512,64]{1,2,0:T(8,128)(2,1)S(1)} %collective-permute-done.5), channel_id=1, source_target_pairs={{1,0},{4,1},{5,4},{8,5},{9,8},{12,9},{13,12},{0,13},{3,2},{6,3},{7... | collective-permute-start | bytes 589832 | tf_op jit(solution)/shard_map/ppermute | solution.py:28
  49.2 12.6 %collective-permute-done.11 = bf16[3,512,64]{1,2,0:T(8,128)(2,1)S(1)} collective-permute-done((bf16[3,512,64]{1,2,0:T(8,128)(2,1)S(1)}, bf16[3,512,64]{1,2,0:T(8,128)(2,1)S(1)}, u32[]{:S(2)}, u32[]{:S(2)}) %collective-permute-start.11) | collective-permute-done | bytes 196640 | tf_op jit(solution)/shard_map/ppermute | solution.py:23
  61.8 7.9 %collective-permute-done.3 = bf16[3,512,64]{1,2,0:T(8,128)(2,1)S(1)} collective-permute-done((bf16[3,512,64]{1,2,0:T(8,128)(2,1)S(1)}, bf16[3,512,64]{1,2,0:T(8,128)(2,1)S(1)}, u32[]{:S(2)}, u32[]{:S(2)}) %collective-permute-start.3) | collective-permute-done | bytes 196640 | tf_op jit(solution)/shard_map/ppermute | solution.py:23
  69.7 2.1 collective-permute-start
  71.8 4.0 %collective-permute-start.7 = (bf16[3,512,64]{1,2,0:T(8,128)(2,1)S(1)}, bf16[3,512,64]{1,2,0:T(8,128)(2,1)S(1)}, u32[]{:S(2)}, u32[]{:S(2)}) collective-permute-start(bf16[3,512,64]{1,2,0:T(8,128)(2,1)S(1)} %collective-permute-done.6), channel_id=1, source_target_pairs={{1,0},{4,1},{5,4},{8,5},{9,8},{12,9},{13,12},{0,13},{3,2},{6,3},{7... | collective-permute-start | bytes 589832 | tf_op jit(solution)/shard_map/ppermute | solution.py:28
  81.3 8.5 %collective-permute-done.13 = bf16[3,512,64]{1,2,0:T(8,128)(2,1)S(1)} collective-permute-done((bf16[3,512,64]{1,2,0:T(8,128)(2,1)S(1)}, bf16[3,512,64]{1,2,0:T(8,128)(2,1)S(1)}, u32[]{:S(2)}, u32[]{:S(2)}) %collective-permute-start.13) | collective-permute-done | bytes 196640 | tf_op jit(solution)/shard_map/ppermute | solution.py:23
  103.0 2.1 gather_fusion.1
  106.7 2.4 multiply_reduce_fusion.3
  109.1 38.4 %all-gather.9.cloned.1.call-done = bf16[1,512,2048]{2,1,0:T(8,128)(2,1)} async-done(((bf16[1,512,256]{2,1,0:T(8,128)(2,1)}), bf16[1,512,2048]{2,1,0:T(8,128)(2,1)}) %all-gather.9.cloned.1.call-update) | async-done | bytes 2097168 | tf_op jit(solution)/shard_map/all_gather | solution.py:84
  147.4 4.8 %multiply_reduce_fusion.2 = (f32[384]{0:T(512)S(1)}, f32[384,512]{1,0:T(8,128)S(1)}) fusion(f32[384,512]{1,0:T(8,128)} %get-tuple-element.24, bf16[1,2048,512]{2,1,0:T(8,128)(2,1)} %all-gather.11.cloned.1.call-done, bf16[1,512,2048]{2,1,0:T(8,128)(2,1)} %all-gather.9.cloned.1.call-done, f32[512]{0:T(512)S(1)} %bitcast.125, f32[384]{0:T(512)S(1)} %add_rsqrt_fusion.3), kind=kOutput, calls=%fused_computation.64 | convolution fusion | flops 1618869888 | bytes 5772288 | tf_op jit(solution)/shard_map/dot_general | solution.py:56
  153.8 5.5 %collective-permute-start.9 = (bf16[384,512]{1,0:T(8,128)(2,1)S(1)}, bf16[384,512]{1,0:T(8,128)(2,1)S(1)}, u32[]{:S(2)}, u32[]{:S(2)}) collective-permute-start(bf16[384,512]{1,0:T(8,128)(2,1)S(1)} %multiply_convert_fusion.4), channel_id=1, source_target_pairs={{0,8},{4,12},{1,9},{5,13},{2,10},{6,14},{3,11},{7,15},{16,24},{20,... | collective-permute-start | bytes 1179656 | tf_op jit(solution)/shard_map/ppermute | solution.py:44
  159.7 21.6 %collective-permute-done.17 = bf16[384,512]{1,0:T(8,128)(2,1)S(1)} collective-permute-done((bf16[384,512]{1,0:T(8,128)(2,1)S(1)}, bf16[384,512]{1,0:T(8,128)(2,1)S(1)}, u32[]{:S(2)}, u32[]{:S(2)}) %collective-permute-start.17) | collective-permute-done | bytes 393248 | tf_op jit(solution)/shard_map/ppermute | solution.py:44
  182.3 26.0 %all-gather.13.cloned.1.call-done = bf16[1,512,2048]{2,1,0:T(8,128)(2,1)} async-done(((bf16[1,512,256]{2,1,0:T(8,128)(2,1)}), bf16[1,512,2048]{2,1,0:T(8,128)(2,1)}) %all-gather.13.cloned.1.call-update) | async-done | bytes 2097168 | tf_op jit(solution)/shard_map/all_gather | solution.py:84
  208.3 49.5 %all-gather.15.cloned.1.call-done = bf16[1,2048,512]{2,1,0:T(8,128)(2,1)} async-done(((bf16[1,256,512]{2,1,0:T(8,128)(2,1)}), bf16[1,2048,512]{2,1,0:T(8,128)(2,1)}) %all-gather.15.cloned.1.call-update) | async-done | bytes 2097168 | tf_op jit(solution)/shard_map/all_gather | solution.py:87
  257.8 4.4 %multiply_reduce_fusion = (f32[384]{0:T(512)S(1)}, f32[384,512]{1,0:T(8,128)S(1)}) fusion(f32[384,512]{1,0:T(8,128)S(1)} %get-tuple-element.28, bf16[1,2048,512]{2,1,0:T(8,128)(2,1)} %all-gather.15.cloned.1.call-done, bf16[1,512,2048]{2,1,0:T(8,128)(2,1)} %all-gather.13.cloned.1.call-done, f32[512]{0:T(512)S(1)} %bitcast.124, f32[384]{0:T(512)S(1)} %add_rsqrt_fusion.1), kind=kOutput, calls=%fused_computation.60 | convolution fusion | flops 1618869888 | bytes 5772288 | tf_op jit(solution)/shard_map/dot_general | solution.py:56
  264.7 10.6 %collective-permute-done.19 = bf16[384,512]{1,0:T(8,128)(2,1)S(1)} collective-permute-done((bf16[384,512]{1,0:T(8,128)(2,1)S(1)}, bf16[384,512]{1,0:T(8,128)(2,1)S(1)}, u32[]{:S(2)}, u32[]{:S(2)}) %collective-permute-start.19) | collective-permute-done | bytes 393248 | tf_op jit(solution)/shard_map/ppermute | solution.py:48
  276.8 8.8 %collective-permute-done.20 = bf16[384,512]{1,0:T(8,128)(2,1)S(1)} collective-permute-done((bf16[384,512]{1,0:T(8,128)(2,1)S(1)}, bf16[384,512]{1,0:T(8,128)(2,1)S(1)}, u32[]{:S(2)}, u32[]{:S(2)}) %collective-permute-start.20) | collective-permute-done | bytes 393248 | tf_op jit(solution)/shard_map/ppermute | solution.py:48
  287.4 16.9 %collective-permute-done.21 = bf16[384,512]{1,0:T(8,128)(2,1)S(1)} collective-permute-done((bf16[384,512]{1,0:T(8,128)(2,1)S(1)}, bf16[384,512]{1,0:T(8,128)(2,1)S(1)}, u32[]{:S(2)}, u32[]{:S(2)}) %collective-permute-start.21) | collective-permute-done | bytes 393248 | tf_op jit(solution)/shard_map/ppermute | solution.py:48
  (98 shorter events, 40.1 us)
Async XLA Ops:
  6.5 102.5 %all-gather.11.cloned.1.call-start = ((), (), s32[]{:S(2)}) async-start(), calls=%async_computation.1 | async-start | bytes 2359296 | tf_op jit(solution)/shard_map/all_gather | solution.py:87
  8.6 138.9 %all-gather.9.cloned.1.call-start = ((), (), s32[]{:S(2)}) async-start(), calls=%async_computation | async-start | bytes 2359296 | tf_op jit(solution)/shard_map/all_gather | solution.py:84
  9.5 198.8 %all-gather.13.cloned.1.call-start = ((), (), s32[]{:S(2)}) async-start(), calls=%async_computation.2 | async-start | bytes 2359296 | tf_op jit(solution)/shard_map/all_gather | solution.py:84
  10.2 247.6 %all-gather.15.cloned.1.call-start = ((), (), s32[]{:S(2)}) async-start(), calls=%async_computation.3 | async-start | bytes 2359296 | tf_op jit(solution)/shard_map/all_gather | solution.py:87
  10.3 19.5 %collective-permute-start.1 = (bf16[3,512,64]{1,2,0:T(8,128)(2,1)S(1)}, bf16[3,512,64]{1,2,0:T(8,128)(2,1)S(1)}, u32[]{:S(2)}, u32[]{:S(2)}) collective-permute-start(bf16[3,512,64]{1,2,0:T(8,128)(2,1)S(1)} %get-tuple-element.18), channel_id=1, source_target_pairs={{0,1},{1,4},{4,5},{5,8},{8,9},{9,12},{12,13},{13,0},{2,3},{3,6},{6... | collective-permute-start | bytes 589832 | tf_op jit(solution)/shard_map/ppermute | solution.py:23
  13.3 31.0 %collective-permute-start.5 = (bf16[3,512,64]{1,2,0:T(8,128)(2,1)S(1)}, bf16[3,512,64]{1,2,0:T(8,128)(2,1)S(1)}, u32[]{:S(2)}, u32[]{:S(2)}) collective-permute-start(bf16[3,512,64]{1,2,0:T(8,128)(2,1)S(1)} %get-tuple-element.18), channel_id=1, source_target_pairs={{1,0},{4,1},{5,4},{8,5},{9,8},{12,9},{13,12},{0,13},{3,2},{6,3},{7... | collective-permute-start | bytes 589832 | tf_op jit(solution)/shard_map/ppermute | solution.py:28
  16.4 18.1 %collective-permute-start.10 = (bf16[3,512,64]{1,2,0:T(8,128)(2,1)S(1)}, bf16[3,512,64]{1,2,0:T(8,128)(2,1)S(1)}, u32[]{:S(2)}, u32[]{:S(2)}) collective-permute-start(bf16[3,512,64]{1,2,0:T(8,128)(2,1)S(1)} %get-tuple-element.17), channel_id=1, source_target_pairs={{0,1},{1,4},{4,5},{5,8},{8,9},{9,12},{12,13},{13,0},{2,3},{3,6},{6... | collective-permute-start | bytes 589832 | tf_op jit(solution)/shard_map/ppermute | solution.py:23
  16.4 32.7 %collective-permute-start.14 = (bf16[3,512,64]{1,2,0:T(8,128)(2,1)S(1)}, bf16[3,512,64]{1,2,0:T(8,128)(2,1)S(1)}, u32[]{:S(2)}, u32[]{:S(2)}) collective-permute-start(bf16[3,512,64]{1,2,0:T(8,128)(2,1)S(1)} %get-tuple-element.17), channel_id=1, source_target_pairs={{1,0},{4,1},{5,4},{8,5},{9,8},{12,9},{13,12},{0,13},{3,2},{6,3},{7... | collective-permute-start | bytes 589832 | tf_op jit(solution)/shard_map/ppermute | solution.py:28
  29.9 14.5 %collective-permute-start.2 = (bf16[3,512,64]{1,2,0:T(8,128)(2,1)S(1)}, bf16[3,512,64]{1,2,0:T(8,128)(2,1)S(1)}, u32[]{:S(2)}, u32[]{:S(2)}) collective-permute-start(bf16[3,512,64]{1,2,0:T(8,128)(2,1)S(1)} %collective-permute-done.1), channel_id=1, source_target_pairs={{0,1},{1,4},{4,5},{5,8},{8,9},{9,12},{12,13},{13,0},{2,3},{3,6},{6... | collective-permute-start | bytes 589832 | tf_op jit(solution)/shard_map/ppermute | solution.py:23
  33.3 66.0 %collective-permute-start.8 = (bf16[384,512]{1,0:T(8,128)(2,1)}, bf16[384,512]{1,0:T(8,128)(2,1)}, u32[]{:S(2)}, u32[]{:S(2)}) collective-permute-start(bf16[384,512]{1,0:T(8,128)(2,1)} %fusion.57), channel_id=1, source_target_pairs={{4,0},{8,4},{12,8},{5,1},{9,5},{13,9},{6,2},{10,6},{14,10},{7,3},{... | collective-permute-start | bytes 1179656 | tf_op jit(solution)/shard_map/ppermute | solution.py:44
  34.6 27.2 %collective-permute-start.11 = (bf16[3,512,64]{1,2,0:T(8,128)(2,1)S(1)}, bf16[3,512,64]{1,2,0:T(8,128)(2,1)S(1)}, u32[]{:S(2)}, u32[]{:S(2)}) collective-permute-start(bf16[3,512,64]{1,2,0:T(8,128)(2,1)S(1)} %collective-permute-done.10), channel_id=1, source_target_pairs={{0,1},{1,4},{4,5},{5,8},{8,9},{9,12},{12,13},{13,0},{2,3},{3,6},{6... | collective-permute-start | bytes 589832 | tf_op jit(solution)/shard_map/ppermute | solution.py:23
  44.3 25.3 %collective-permute-start.3 = (bf16[3,512,64]{1,2,0:T(8,128)(2,1)S(1)}, bf16[3,512,64]{1,2,0:T(8,128)(2,1)S(1)}, u32[]{:S(2)}, u32[]{:S(2)}) collective-permute-start(bf16[3,512,64]{1,2,0:T(8,128)(2,1)S(1)} %collective-permute-done.2), channel_id=1, source_target_pairs={{0,1},{1,4},{4,5},{5,8},{8,9},{9,12},{12,13},{13,0},{2,3},{3,6},{6... | collective-permute-start | bytes 589832 | tf_op jit(solution)/shard_map/ppermute | solution.py:23
  44.4 25.3 %collective-permute-start.6 = (bf16[3,512,64]{1,2,0:T(8,128)(2,1)S(1)}, bf16[3,512,64]{1,2,0:T(8,128)(2,1)S(1)}, u32[]{:S(2)}, u32[]{:S(2)}) collective-permute-start(bf16[3,512,64]{1,2,0:T(8,128)(2,1)S(1)} %collective-permute-done.5), channel_id=1, source_target_pairs={{1,0},{4,1},{5,4},{8,5},{9,8},{12,9},{13,12},{0,13},{3,2},{6,3},{7... | collective-permute-start | bytes 589832 | tf_op jit(solution)/shard_map/ppermute | solution.py:28
  49.1 22.6 %collective-permute-start.15 = (bf16[3,512,64]{1,2,0:T(8,128)(2,1)S(1)}, bf16[3,512,64]{1,2,0:T(8,128)(2,1)S(1)}, u32[]{:S(2)}, u32[]{:S(2)}) collective-permute-start(bf16[3,512,64]{1,2,0:T(8,128)(2,1)S(1)} %collective-permute-done.14), channel_id=1, source_target_pairs={{1,0},{4,1},{5,4},{8,5},{9,8},{12,9},{13,12},{0,13},{3,2},{6,3},{7... | collective-permute-start | bytes 589832 | tf_op jit(solution)/shard_map/ppermute | solution.py:28
  61.8 14.0 %collective-permute-start.12 = (bf16[3,512,64]{1,2,0:T(8,128)(2,1)S(1)}, bf16[3,512,64]{1,2,0:T(8,128)(2,1)S(1)}, u32[]{:S(2)}, u32[]{:S(2)}) collective-permute-start(bf16[3,512,64]{1,2,0:T(8,128)(2,1)S(1)} %collective-permute-done.11), channel_id=1, source_target_pairs={{0,1},{1,4},{4,5},{5,8},{8,9},{9,12},{12,13},{13,0},{2,3},{3,6},{6... | collective-permute-start | bytes 589832 | tf_op jit(solution)/shard_map/ppermute | solution.py:23
  69.7 37.0 %collective-permute-start = (bf16[384,512]{1,0:T(8,128)(2,1)}, bf16[384,512]{1,0:T(8,128)(2,1)}, u32[]{:S(2)}, u32[]{:S(2)}) collective-permute-start(bf16[384,512]{1,0:T(8,128)(2,1)} %fusion.57), channel_id=1, source_target_pairs={{0,4},{4,8},{8,12},{1,5},{5,9},{9,13},{2,6},{6,10},{10,14},{3,7},{... | collective-permute-start | bytes 1179656 | tf_op jit(solution)/shard_map/ppermute | solution.py:44
  71.8 23.7 %collective-permute-start.7 = (bf16[3,512,64]{1,2,0:T(8,128)(2,1)S(1)}, bf16[3,512,64]{1,2,0:T(8,128)(2,1)S(1)}, u32[]{:S(2)}, u32[]{:S(2)}) collective-permute-start(bf16[3,512,64]{1,2,0:T(8,128)(2,1)S(1)} %collective-permute-done.6), channel_id=1, source_target_pairs={{1,0},{4,1},{5,4},{8,5},{9,8},{12,9},{13,12},{0,13},{3,2},{6,3},{7... | collective-permute-start | bytes 589832 | tf_op jit(solution)/shard_map/ppermute | solution.py:28
  75.8 25.6 %collective-permute-start.16 = (bf16[3,512,64]{1,2,0:T(8,128)(2,1)S(1)}, bf16[3,512,64]{1,2,0:T(8,128)(2,1)}, u32[]{:S(2)}, u32[]{:S(2)}) collective-permute-start(bf16[3,512,64]{1,2,0:T(8,128)(2,1)S(1)} %collective-permute-done.15), channel_id=1, source_target_pairs={{1,0},{4,1},{5,4},{8,5},{9,8},{12,9},{13,12},{0,13},{3,2},{6,3},{7... | collective-permute-start | bytes 589832 | tf_op jit(solution)/shard_map/ppermute | solution.py:28
  78.5 11.3 %collective-permute-start.13 = (bf16[3,512,64]{1,2,0:T(8,128)(2,1)S(1)}, bf16[3,512,64]{1,2,0:T(8,128)(2,1)S(1)}, u32[]{:S(2)}, u32[]{:S(2)}) collective-permute-start(bf16[3,512,64]{1,2,0:T(8,128)(2,1)S(1)} %collective-permute-done.12), channel_id=1, source_target_pairs={{0,1},{1,4},{4,5},{5,8},{8,9},{9,12},{12,13},{13,0},{2,3},{3,6},{6... | collective-permute-start | bytes 589832 | tf_op jit(solution)/shard_map/ppermute | solution.py:23
  152.4 28.9 %collective-permute-start.17 = (bf16[384,512]{1,0:T(8,128)(2,1)S(1)}, bf16[384,512]{1,0:T(8,128)(2,1)S(1)}, u32[]{:S(2)}, u32[]{:S(2)}) collective-permute-start(bf16[384,512]{1,0:T(8,128)(2,1)S(1)} %multiply_convert_fusion.4), channel_id=1, source_target_pairs={{8,0},{12,4},{9,1},{13,5},{10,2},{14,6},{11,3},{15,7},{24,16},{28,... | collective-permute-start | bytes 1179656 | tf_op jit(solution)/shard_map/ppermute | solution.py:44
  153.8 27.9 %collective-permute-start.9 = (bf16[384,512]{1,0:T(8,128)(2,1)S(1)}, bf16[384,512]{1,0:T(8,128)(2,1)S(1)}, u32[]{:S(2)}, u32[]{:S(2)}) collective-permute-start(bf16[384,512]{1,0:T(8,128)(2,1)S(1)} %multiply_convert_fusion.4), channel_id=1, source_target_pairs={{0,8},{4,12},{1,9},{5,13},{2,10},{6,14},{3,11},{7,15},{16,24},{20,... | collective-permute-start | bytes 1179656 | tf_op jit(solution)/shard_map/ppermute | solution.py:44
  264.1 11.2 %collective-permute-start.19 = (bf16[384,512]{1,0:T(8,128)(2,1)S(1)}, bf16[384,512]{1,0:T(8,128)(2,1)S(1)}, u32[]{:S(2)}, u32[]{:S(2)}) collective-permute-start(bf16[384,512]{1,0:T(8,128)(2,1)S(1)} %collective-permute-done.18), channel_id=1, source_target_pairs={{0,1},{1,0},{4,5},{5,4},{8,9},{9,8},{12,13},{13,12},{2,3},{3,2},{6... | collective-permute-start | bytes 1179656 | tf_op jit(solution)/shard_map/ppermute | solution.py:48
  275.3 10.3 %collective-permute-start.20 = (bf16[384,512]{1,0:T(8,128)(2,1)S(1)}, bf16[384,512]{1,0:T(8,128)(2,1)S(1)}, u32[]{:S(2)}, u32[]{:S(2)}) collective-permute-start(bf16[384,512]{1,0:T(8,128)(2,1)S(1)} %collective-permute-done.19), channel_id=1, source_target_pairs={{0,4},{1,5},{4,0},{5,1},{8,12},{9,13},{12,8},{13,9},{2,6},{3,7},{6... | collective-permute-start | bytes 1179656 | tf_op jit(solution)/shard_map/ppermute | solution.py:48
  285.6 18.7 %collective-permute-start.21 = (bf16[384,512]{1,0:T(8,128)(2,1)S(1)}, bf16[384,512]{1,0:T(8,128)(2,1)S(1)}, u32[]{:S(2)}, u32[]{:S(2)}) collective-permute-start(bf16[384,512]{1,0:T(8,128)(2,1)S(1)} %collective-permute-done.20), channel_id=1, source_target_pairs={{0,8},{1,9},{4,12},{5,13},{8,0},{9,1},{12,4},{13,5},{2,10},{3,11},... | collective-permute-start | bytes 1179656 | tf_op jit(solution)/shard_map/ppermute | solution.py:48
  (12 other events, 408.5 us)
Sparse Core Ops, SparseCore 0:
  9.5 82.5 all-gather.10
  94.1 53.2 all-gather.8
  149.5 58.7 all-gather.12
  210.3 47.4 all-gather.14
